TPU v7x, 256 devices: a whole 4x4x8 slice. The times are simulated.
256 devices in a mesh: task: 8 (over x_hi, y), mp: 32 (over x_lo, z, core).
Axes of the slice: x: 4 (x_hi: 2, x_lo: 2; x = x_hi * 2 + x_lo), y: 4, z: 8, core: 2. Of those that a mesh axis runs over, the one named last changes fastest.
Arguments:
- hidden: bfloat16 [8, 2048, 8192], P('task', 'mp'), may hold values from -6 to 6
- gain: float32 [8192], replicated, may hold values from 0.25 to 1.75
- tau: bfloat16 [8, 8192, 1024], P('task', 'mp'), may hold values from -0.0625 to 0.0625
- coeff: float32 [8, 8192, 1024], P('task', 'mp'), may hold values from 0.1 to 1
- counts: int32 [8], P('task'), may hold values from 683 to 2048, as said below
- positions: int32 [8, 2048], P('task', 'mp'), may hold values from 0 to 2047
Outputs:
- grad_coeff: float32 [8, 8192, 1024], P('task', 'mp')
- loss: float32 [], replicated
Inputs may be any that keep to these rules, and one draw needn't show every extreme that they name: `counts`: counts lie between a third of 2048 and 2048; some task has exactly 2048 in every draw. Rows at or past a task's count are not live.
All inputs are finite; a program needn't handle non-finite values.
Results may differ from a plain program's by a relative error of at most 0.0044.
The roundings to bfloat16 on the way count: a program that leaves them out, or rounds other values in their place, can miss the bound.
Values may be sent and summed in bfloat16 or wider, within the bound.
A program may use at most 64 MiB of HBM per device.

v0:
```python
import jax
import jax.numpy as jnp
from jax import lax
from jax.sharding import Mesh
from jax.sharding import PartitionSpec as P

HEAD = 128
MP = ("mp_0", "mp_1", "mp_2")
TASK = ("task_0", "task_1")
TASK_MP = ("task_0", "task_1", "mp_0", "mp_1", "mp_2")


def cut_along(value, dim, length):
    before, after = (value.shape[:dim], value.shape[dim + 1 :])
    return jnp.moveaxis(value.reshape(*before, length, -1, *after), dim, 0)


def scatter_pairs(value, chips, core, dim):
    sizes = (lax.axis_size(chips), lax.axis_size(core))
    tiles = cut_along(value, dim, sizes[0] * sizes[1])
    inside = tiles.shape[1:]
    tiles = tiles.reshape(*sizes, *inside).swapaxes(0, 1).reshape(-1, *inside)
    tiles = lax.psum_scatter(tiles, core, scatter_dimension=0, tiled=True)
    return lax.psum_scatter(tiles, chips, scatter_dimension=0, tiled=True)[0]


def by_axis(value, axes):
    for axis in axes:
        value = lax.psum(value, axis)
    return value


def rotary_tables(positions, head):
    index = jnp.arange(head // 2).astype(jnp.float32)
    freq = jnp.exp(-jnp.log(jnp.float32(1000000.0)) * 2.0 * index / head)
    angle = positions.astype(jnp.float32)[:, None] * freq[None, :]
    return (jnp.cos(angle), jnp.sin(angle))


def rotate(values, cosine, sine, sign, head):
    count = values.shape[0]
    width = values.shape[1]
    shaped = values.reshape(count, width // head, 2, head // 2)
    first = shaped[:, :, 0, :]
    second = shaped[:, :, 1, :]
    cosine = cosine[:, None, :]
    sine = sine[:, None, :] * sign
    out_first = first * cosine - second * sine
    out_second = second * cosine + first * sine
    return jnp.stack([out_first, out_second], axis=2).reshape(count, width)


def local(hidden, gain, tau, coeff, counts, positions):
    rows = hidden[0].astype(jnp.float32)
    width = rows.shape[1]
    keys = tau.shape[2]
    rows_local = rows.shape[0]
    inverse = 1.0 / jnp.sqrt(jnp.mean(rows * rows, axis=1, keepdims=True) + 1e-06)
    normed = (rows * inverse * gain[None, :]).astype(jnp.bfloat16)
    columns = lax.all_to_all(normed, MP, split_axis=1, concat_axis=0, tiled=True)
    tau_local = tau[0].astype(jnp.float32)
    mixed = lax.psum(coeff[0] * tau_local, TASK)
    merged = mixed.astype(jnp.bfloat16)
    teacher = tau[0]
    block = columns
    gap = scatter_pairs(
        jnp.dot(block, merged, preferred_element_type=jnp.float32)
        - jnp.dot(block, teacher, preferred_element_type=jnp.float32),
        ("mp_0", "mp_1"),
        "mp_2",
        0,
    )
    first_row = lax.axis_index(MP) * rows_local
    cosine, sine = rotary_tables(positions[0], HEAD)
    err = rotate(gap, cosine, sine, 1.0, HEAD)
    row_ids = first_row + jnp.arange(rows_local)
    live = (row_ids < counts[0]).astype(jnp.float32)[:, None]
    scale = 1.0 / (counts[0].astype(jnp.float32) * keys)
    partial_loss = jnp.sum(live * err * err) * scale
    back = rotate(2.0 * scale * live * err, cosine, sine, -1.0, HEAD).astype(jnp.bfloat16)
    block = columns
    local_grad = lax.dot_general(
        block,
        lax.all_gather(back, MP, axis=0, tiled=True),
        (((0,), (0,)), ((), ())),
        preferred_element_type=jnp.float32,
    )
    wgrad = lax.psum(local_grad, TASK)
    loss = by_axis(partial_loss, TASK_MP)
    grad_coeff = width * keys * tau_local * wgrad
    return (grad_coeff[None, :, :], loss)


def solution(mesh):
    split = Mesh(mesh.devices.reshape(2, 4, 2, 8, 2), ("task_0", "task_1", "mp_0", "mp_1", "mp_2"))
    placed = (P(TASK, MP, None), P(), P(TASK, MP, None), P(TASK, MP, None), P(TASK), P(TASK, MP))
    return jax.shard_map(
        local, mesh=split, in_specs=placed, out_specs=(P(TASK, MP, None), P()), check_vma=False
    )
```

profile of v0, /device:TPU:32, one launch (start us, length us, event | category | flops | bytes accessed | tf_op | source)
XLA Modules:
  0.0 391.9 jit_solution(13827501548182623606)
XLA Ops:
  7.2 0.0 copy-start.1
  7.2 1.5 multiply_reduce_fusion
  8.7 1.5 copy.13
  10.2 0.0 copy-done.1
  10.2 0.0 copy-start
  10.3 0.3 fusion.1
  10.6 1.6 copy.11
  12.1 9.7 %all-to-all-start = ((bf16[64,32,256]{2,0,1:T(8,128)(2,1)}), bf16[64,32,256]{2,0,1:T(8,128)(2,1)S(1)}, u32[]{:S(2)}, u32[]{:S(2)}) async-start(bf16[64,32,256]{2,0,1:T(8,128)(2,1)} %copy.11), calls=%async_computation | async-start | bytes 2097152 | tf_op jit(solution)/shard_map/all_to_all | solution.py:60
  21.8 0.0 reduce-scatter.3.cloned.1.call-start
  21.8 0.0 copy-done
  21.8 1.4 convert_multiply_fusion
  23.2 81.8 %all-reduce.4 = bf16[256,1024]{1,0:T(8,128)(2,1)S(1)} all-reduce(f32[256,1024]{1,0:T(8,128)S(1)} %convert_multiply_fusion), channel_id=1, replica_groups=mesh['task_0'=2,'task_1'=4,'mp_0'=2,'mp_1'=8,'mp_2'=2] {'task_0','task_1'}, use_global_device_ids=true, to_apply=%region_1.0 | all-reduce | flops 262144 | bytes 1572864 | tf_op jit(solution)/shard_map/psum | solution.py:62
  105.0 0.0 all-to-all-done
  105.0 1.3 fusion.9
  106.3 1.3 convolution_subtract_fusion
  107.6 4.1 %copy.12 = f32[16,2,64,1024]{3,2,0,1:T(8,128)} copy(f32[16,2,64,1024]{3,2,1,0:T(8,128)S(1)} %bitcast.36) | data formatting | bytes 16777216 | tf_op jit(solution)/shard_map/reshape;reshape | solution.py:22
  111.6 0.0 reduce-scatter.3.cloned.1.call-update
  111.7 0.0 copy-start.2
  111.7 0.0 reduce-scatter.5.cloned.1.call-start
  111.7 19.8 %reduce-scatter.3.cloned.1.call-done = f32[16,64,1024]{2,1,0:T(8,128)} async-done(((f32[32,64,1024]{2,1,0:T(8,128)}), f32[16,64,1024]{2,1,0:T(8,128)}) %reduce-scatter.3.cloned.1.call-update) | async-done | bytes 4194320 | tf_op jit(solution)/shard_map/reduce_scatter | solution.py:23
  131.5 0.0 reduce-scatter.5.cloned.1.call-update
  131.6 0.0 all-gather.2.cloned.1.call-start
  132.4 0.0 copy-done.2
  132.4 0.2 broadcast_multiply_fusion.1
  132.6 81.7 %reduce-scatter.5.cloned.1.call-done = f32[1,64,1024]{2,1,0:T(8,128)} async-done(((f32[16,64,1024]{2,1,0:T(8,128)}), f32[1,64,1024]{2,1,0:T(8,128)}) %reduce-scatter.5.cloned.1.call-update) | async-done | bytes 262160 | tf_op jit(solution)/shard_map/reduce_scatter | solution.py:24
  214.2 1.3 reshape_squeeze.3
  215.6 0.6 multiply_subtract_fusion
  216.2 1.8 fusion.4
  217.9 0.7 subtract_convert_fusion
  218.6 0.7 pad_maximum_fusion.1
  219.3 0.9 convert_element_type.62
  220.2 0.0 all-gather.2.cloned.1.call-update
  220.2 0.0 all-reduce.3.cloned.1.call-start
  220.3 64.3 %all-gather.2.cloned.1.call-done = bf16[2048,1024]{1,0:T(8,128)(2,1)} async-done(((bf16[64,1024]{1,0:T(8,128)(2,1)}), bf16[2048,1024]{1,0:T(8,128)(2,1)}) %all-gather.2.cloned.1.call-update) | async-done | bytes 4194320 | tf_op jit(solution)/shard_map/all_gather | solution.py:84
  284.5 4.4 %fusion.8 = f32[256,1024]{1,0:T(8,128)} fusion(bf16[2048,256]{1,0:T(8,128)(2,1)S(1)} %bitcast.40, bf16[2048,1024]{1,0:T(8,128)(2,1)} %all-gather.2.cloned.1.call-done), kind=kOutput, calls=%fused_computation.30 | convolution fusion | flops 1073741824 | bytes 6291456 | tf_op jit(solution)/shard_map/dot_general | solution.py:82
  289.0 0.0 all-reduce.3.cloned.1.call-update
  289.6 6.9 %psum.51 = f32[]{:T(128)} all-reduce(f32[]{:T(128)S(6)} %mul.221), channel_id=1, replica_groups=mesh['task_0'=2,'task_1'=4,'mp_0'=2,'mp_1'=8,'mp_2'=2] {'task_0'}, use_global_device_ids=true, to_apply=%region_6.0 | all-reduce | flops 1 | bytes 8 | tf_op jit(solution)/shard_map/psum | solution.py:29
  296.6 11.5 %psum.52 = f32[]{:T(128)} all-reduce(f32[]{:T(128)} %psum.51), channel_id=1, replica_groups=mesh['task_0'=2,'task_1'=4,'mp_0'=2,'mp_1'=8,'mp_2'=2] {'task_1'}, use_global_device_ids=true, to_apply=%region_7.0 | all-reduce | flops 1 | bytes 8 | tf_op jit(solution)/shard_map/psum | solution.py:29
  308.1 5.5 %psum.53 = f32[]{:T(128)} all-reduce(f32[]{:T(128)} %psum.52), channel_id=1, replica_groups=mesh['task_0'=2,'task_1'=4,'mp_0'=2,'mp_1'=8,'mp_2'=2] {'mp_0'}, use_global_device_ids=true, to_apply=%region_8.0 | all-reduce | flops 1 | bytes 8 | tf_op jit(solution)/shard_map/psum | solution.py:29
  313.6 15.9 %psum.54 = f32[]{:T(128)} all-reduce(f32[]{:T(128)} %psum.53), channel_id=1, replica_groups=mesh['task_0'=2,'task_1'=4,'mp_0'=2,'mp_1'=8,'mp_2'=2] {'mp_1'}, use_global_device_ids=true, to_apply=%region_9.0 | all-reduce | flops 1 | bytes 8 | tf_op jit(solution)/shard_map/psum | solution.py:29
  329.5 3.1 psum.55
  332.5 50.5 %all-reduce.3.cloned.1.call-done = f32[256,1024]{1,0:T(8,128)} async-done(((f32[256,1024]{1,0:T(8,128)}), f32[256,1024]{1,0:T(8,128)}) %all-reduce.3.cloned.1.call-update) | async-done | bytes 1048592 | tf_op jit(solution)/shard_map/psum | solution.py:88
  383.0 2.4 fusion.3
  (6 shorter events, 0.0 us)
Async XLA Ops:
  7.2 3.1 copy-start.1
  10.2 11.6 %copy-start = (bf16[1,256,1024]{2,1,0:T(8,128)(2,1)S(1)}, bf16[1,256,1024]{2,1,0:T(8,128)(2,1)}, u32[]{:S(2)}) copy-start(bf16[1,256,1024]{2,1,0:T(8,128)(2,1)} %param.8) | copy-start | bytes 1572868
  12.1 92.9 %all-to-all-start = ((bf16[64,32,256]{2,0,1:T(8,128)(2,1)}), bf16[64,32,256]{2,0,1:T(8,128)(2,1)S(1)}, u32[]{:S(2)}, u32[]{:S(2)}) async-start(bf16[64,32,256]{2,0,1:T(8,128)(2,1)} %copy.11), calls=%async_computation | async-start | bytes 2097152 | tf_op jit(solution)/shard_map/all_to_all | solution.py:60
  21.8 109.8 %reduce-scatter.3.cloned.1.call-start = ((), (), s32[]{:S(2)}) async-start(), calls=%async_computation.3 | async-start | bytes 12582912 | tf_op jit(solution)/shard_map/reduce_scatter | solution.py:23
  111.7 20.7 %copy-start.2 = (s32[1,64]{1,0:T(1,128)S(1)}, s32[1,64]{1,0:T(1,128)}, u32[]{:S(2)}) copy-start(s32[1,64]{1,0:T(1,128)} %param.11) | copy-start | bytes 772
  111.7 102.6 %reduce-scatter.5.cloned.1.call-start = ((), (), s32[]{:S(2)}) async-start(), calls=%async_computation.4 | async-start | bytes 4456448 | tf_op jit(solution)/shard_map/reduce_scatter | solution.py:24
  131.6 153.0 %all-gather.2.cloned.1.call-start = ((), (), s32[]{:S(2)}) async-start(), calls=%async_computation.5 | async-start | bytes 4325376 | tf_op jit(solution)/shard_map/all_gather | solution.py:84
  220.2 162.8 %all-reduce.3.cloned.1.call-start = ((), (), s32[]{:S(2)}) async-start(), calls=%async_computation.6 | async-start | bytes 2097152 | tf_op jit(solution)/shard_map/psum | solution.py:88
Sparse Core Ops, SparseCore 0:
  111.8 19.7 reduce-scatter.2
  134.1 80.0 reduce-scatter.4
  220.3 64.1 all-gather.1
  289.1 93.8 all-reduce.2
where the time goes:
time: 392 us
  waiting for transfers between devices  216 us (55%)
  blocking collectives  125 us (32%)
  between operations  15.3 us (4%)
  starting transfers between devices  9.82 us (3%)
  other arithmetic  9.5 us (2%)
  local copies, waits for them, and re-layouts  9.36 us (2%)
  matrix products  6.95 us (2%)
    psum x1, blocking collectives, local(): mixed = lax.psum(coeff[0] * tau_local, TASK)  81.8 us
    reduce_scatter x1, waiting for transfers between devices, scatter_pairs(): return lax.psum_scatter(tiles, chips, scatter_dimension=0, tiled=True)[0]  81.7 us
    all_gather x1, waiting for transfers between devices, local(): lax.all_gather(back, MP, axis=0, tiled=True)  64.3 us
    psum x1, waiting for transfers between devices, local(): wgrad = lax.psum(local_grad, TASK)  50.5 us
    psum x5, blocking collectives, by_axis(): value = lax.psum(value, axis)  42.9 us
    reduce_scatter x1, waiting for transfers between devices, scatter_pairs(): tiles = lax.psum_scatter(tiles, core, scatter_dimension=0, tiled=True)  19.8 us
    all_to_all x1, starting transfers between devices, local(): lax.all_to_all(normed, MP, split_axis=1, concat_axis=0, tiled=True)  9.65 us
  transfers between devices with their start and end apart: 5, of which 4 were waited for; matrix products, arithmetic and copies ran while one was open for 0% of the time, Pallas kernels for 0%

commit v1 on v0

--- a/solution.py
+++ b/solution.py
@@ -85,7 +85,7 @@
         (((0,), (0,)), ((), ())),
         preferred_element_type=jnp.float32,
     )
-    wgrad = lax.psum(local_grad, TASK)
+    wgrad = jnp.sum(lax.all_gather(local_grad, TASK), axis=0)
     loss = by_axis(partial_loss, TASK_MP)
     grad_coeff = width * keys * tau_local * wgrad
     return (grad_coeff[None, :, :], loss)

time: 392 us -> 415 us (1.059)
  waiting for transfers between devices: 216 us -> 235 us
    all_gather x0 -> x1, waiting for transfers between devices: none -> 69.1 us  [local(): wgrad = jnp.sum(lax.all_gather(local_grad, TASK), axis=0)]
    psum x1 -> x0, waiting for transfers between devices: 50.5 us -> none  [local(): wgrad = lax.psum(local_grad, TASK)]
    reduce_sum x0 -> x1, other arithmetic: none -> 4.38 us  [local(): wgrad = jnp.sum(lax.all_gather(local_grad, TASK), axis=0)]
where the time goes in v1:
time: 415 us; the launch traced here: 414 us
  waiting for transfers between devices  235 us (57%)
  blocking collectives  125 us (30%)
  between operations  15.3 us (4%)
  other arithmetic  12.8 us (3%)
  starting transfers between devices  9.82 us (2%)
  local copies, waits for them, and re-layouts  9.36 us (2%)
  matrix products  6.94 us (2%)
    reduce_scatter x1, waiting for transfers between devices, scatter_pairs(): return lax.psum_scatter(tiles, chips, scatter_dimension=0, tiled=True)[0]  82.1 us
    psum x1, blocking collectives, local(): mixed = lax.psum(coeff[0] * tau_local, TASK)  81.7 us
    all_gather x1, waiting for transfers between devices, local(): wgrad = jnp.sum(lax.all_gather(local_grad, TASK), axis=0)  69.1 us
    all_gather x1, waiting for transfers between devices, local(): lax.all_gather(back, MP, axis=0, tiled=True)  64 us
    psum x5, blocking collectives, by_axis(): value = lax.psum(value, axis)  43 us
    reduce_scatter x1, waiting for transfers between devices, scatter_pairs(): tiles = lax.psum_scatter(tiles, core, scatter_dimension=0, tiled=True)  19.9 us
    all_to_all x1, starting transfers between devices, local(): lax.all_to_all(normed, MP, split_axis=1, concat_axis=0, tiled=True)  9.65 us
  transfers between devices with their start and end apart: 5, of which 4 were waited for; matrix products, arithmetic and copies ran while one was open for 0% of the time, Pallas kernels for 0%

profile of v1, /device:TPU:32, one launch (start us, length us, event | category | flops | bytes accessed | tf_op | source)
XLA Modules:
  0.0 414.1 jit_solution(15596810838373076728)
XLA Ops:
  7.2 0.0 copy-start.1
  7.2 1.5 multiply_reduce_fusion
  8.7 1.5 copy.13
  10.2 0.0 copy-done.1
  10.3 0.3 fusion.1
  10.5 1.6 copy.11
  12.1 9.7 %all-to-all-start = ((bf16[64,32,256]{2,0,1:T(8,128)(2,1)}), bf16[64,32,256]{2,0,1:T(8,128)(2,1)S(1)}, u32[]{:S(2)}, u32[]{:S(2)}) async-start(bf16[64,32,256]{2,0,1:T(8,128)(2,1)} %copy.11), calls=%async_computation | async-start | bytes 2097152 | tf_op jit(solution)/shard_map/all_to_all | solution.py:60
  21.8 0.0 reduce-scatter.3.cloned.1.call-start
  21.8 1.5 bitcast_multiply_fusion.2
  23.3 81.7 %all-reduce.1 = bf16[256,1024]{1,0:T(8,128)(2,1)S(1)} all-reduce(f32[256,1024]{1,0:T(8,128)S(1)} %bitcast_multiply_fusion.2), channel_id=1, replica_groups=mesh['task_0'=2,'task_1'=4,'mp_0'=2,'mp_1'=8,'mp_2'=2] {'task_0','task_1'}, use_global_device_ids=true, to_apply=%region_1.0 | all-reduce | flops 262144 | bytes 1572864 | tf_op jit(solution)/shard_map/psum | solution.py:62
  105.0 0.0 all-to-all-done
  105.0 0.0 copy-start
  105.1 1.3 fusion.7
  106.3 0.0 copy-done
  106.3 1.3 convolution_subtract_fusion
  107.6 4.1 copy.12
  111.7 0.0 reduce-scatter.3.cloned.1.call-update
  111.7 0.0 copy-start.2
  111.7 0.0 reduce-scatter.5.cloned.1.call-start
  111.7 19.9 %reduce-scatter.3.cloned.1.call-done = f32[16,64,1024]{2,1,0:T(8,128)} async-done(((f32[32,64,1024]{2,1,0:T(8,128)}), f32[16,64,1024]{2,1,0:T(8,128)}) %reduce-scatter.3.cloned.1.call-update) | async-done | bytes 4194320 | tf_op jit(solution)/shard_map/reduce_scatter | solution.py:23
  131.6 0.0 reduce-scatter.5.cloned.1.call-update
  131.6 0.0 all-gather.4.cloned.1.call-start
  132.4 0.0 copy-done.2
  132.4 0.2 broadcast_multiply_fusion.1
  132.6 82.1 %reduce-scatter.5.cloned.1.call-done = f32[1,64,1024]{2,1,0:T(8,128)} async-done(((f32[16,64,1024]{2,1,0:T(8,128)}), f32[1,64,1024]{2,1,0:T(8,128)}) %reduce-scatter.5.cloned.1.call-update) | async-done | bytes 262160 | tf_op jit(solution)/shard_map/reduce_scatter | solution.py:24
  214.8 1.3 reshape_squeeze.3
  216.1 0.6 multiply_subtract_fusion
  216.7 1.8 fusion.2
  218.5 0.7 subtract_convert_fusion
  219.1 0.7 pad_maximum_fusion.1
  219.9 0.9 convert_element_type.66
  220.7 0.0 all-gather.4.cloned.1.call-update
  220.7 0.0 all-gather.6.cloned.1.call-start
  220.8 64.0 %all-gather.4.cloned.1.call-done = bf16[2048,1024]{1,0:T(8,128)(2,1)} async-done(((bf16[64,1024]{1,0:T(8,128)(2,1)}), bf16[2048,1024]{1,0:T(8,128)(2,1)}) %all-gather.4.cloned.1.call-update) | async-done | bytes 4194320 | tf_op jit(solution)/shard_map/all_gather | solution.py:84
  284.8 4.4 %fusion.6 = f32[256,1024]{1,0:T(8,128)} fusion(bf16[2048,256]{1,0:T(8,128)(2,1)S(1)} %bitcast.40, bf16[2048,1024]{1,0:T(8,128)(2,1)} %all-gather.4.cloned.1.call-done), kind=kOutput, calls=%fused_computation.28 | convolution fusion | flops 1073741824 | bytes 6291456 | tf_op jit(solution)/shard_map/dot_general | solution.py:82
  289.2 0.0 all-gather.6.cloned.1.call-update
  289.9 6.9 %psum.43 = f32[]{:T(128)} all-reduce(f32[]{:T(128)S(6)} %mul.223), channel_id=1, replica_groups=mesh['task_0'=2,'task_1'=4,'mp_0'=2,'mp_1'=8,'mp_2'=2] {'task_0'}, use_global_device_ids=true, to_apply=%region_6.0 | all-reduce | flops 1 | bytes 8 | tf_op jit(solution)/shard_map/psum | solution.py:29
  296.8 11.1 %psum.44 = f32[]{:T(128)} all-reduce(f32[]{:T(128)} %psum.43), channel_id=1, replica_groups=mesh['task_0'=2,'task_1'=4,'mp_0'=2,'mp_1'=8,'mp_2'=2] {'task_1'}, use_global_device_ids=true, to_apply=%region_7.0 | all-reduce | flops 1 | bytes 8 | tf_op jit(solution)/shard_map/psum | solution.py:29
  307.9 5.8 %psum.45 = f32[]{:T(128)} all-reduce(f32[]{:T(128)} %psum.44), channel_id=1, replica_groups=mesh['task_0'=2,'task_1'=4,'mp_0'=2,'mp_1'=8,'mp_2'=2] {'mp_0'}, use_global_device_ids=true, to_apply=%region_8.0 | all-reduce | flops 1 | bytes 8 | tf_op jit(solution)/shard_map/psum | solution.py:29
  313.7 16.2 %psum.46 = f32[]{:T(128)} all-reduce(f32[]{:T(128)} %psum.45), channel_id=1, replica_groups=mesh['task_0'=2,'task_1'=4,'mp_0'=2,'mp_1'=8,'mp_2'=2] {'mp_1'}, use_global_device_ids=true, to_apply=%region_9.0 | all-reduce | flops 1 | bytes 8 | tf_op jit(solution)/shard_map/psum | solution.py:29
  329.8 3.1 psum.47
  332.9 69.1 %all-gather.6.cloned.1.call-done = f32[2048,1024]{1,0:T(8,128)} async-done(((f32[256,1024]{1,0:T(8,128)}), f32[2048,1024]{1,0:T(8,128)}) %all-gather.6.cloned.1.call-update) | async-done | bytes 8388624 | tf_op jit(solution)/shard_map/all_gather | solution.py:88
  402.0 4.4 %reduce_sum.30 = f32[256,1024]{1,0:T(8,128)S(1)} reduce(f32[8,256,1024]{2,1,0:T(8,128)} %bitcast.41, f32[]{:T(128)} %constant.16.clone.1), dimensions={0}, to_apply=%region_4.0 | reduce | flops 1835008 | bytes 9437188 | tf_op jit(solution)/shard_map/reduce_sum | solution.py:88
  406.4 1.2 bitcast_multiply_fusion.1
  (6 shorter events, 0.0 us)
Async XLA Ops:
  7.2 3.1 copy-start.1
  12.1 92.9 %all-to-all-start = ((bf16[64,32,256]{2,0,1:T(8,128)(2,1)}), bf16[64,32,256]{2,0,1:T(8,128)(2,1)S(1)}, u32[]{:S(2)}, u32[]{:S(2)}) async-start(bf16[64,32,256]{2,0,1:T(8,128)(2,1)} %copy.11), calls=%async_computation | async-start | bytes 2097152 | tf_op jit(solution)/shard_map/all_to_all | solution.py:60
  21.8 109.8 %reduce-scatter.3.cloned.1.call-start = ((), (), s32[]{:S(2)}) async-start(), calls=%async_computation.3 | async-start | bytes 12582912 | tf_op jit(solution)/shard_map/reduce_scatter | solution.py:23
  105.0 1.3 copy-start
  111.7 20.7 %copy-start.2 = (s32[1,64]{1,0:T(1,128)S(1)}, s32[1,64]{1,0:T(1,128)}, u32[]{:S(2)}) copy-start(s32[1,64]{1,0:T(1,128)} %param.11) | copy-start | bytes 772
  111.7 103.1 %reduce-scatter.5.cloned.1.call-start = ((), (), s32[]{:S(2)}) async-start(), calls=%async_computation.4 | async-start | bytes 4456448 | tf_op jit(solution)/shard_map/reduce_scatter | solution.py:24
  131.6 153.2 %all-gather.4.cloned.1.call-start = ((), (), s32[]{:S(2)}) async-start(), calls=%async_computation.5 | async-start | bytes 4325376 | tf_op jit(solution)/shard_map/all_gather | solution.py:84
  220.7 181.3 %all-gather.6.cloned.1.call-start = ((), (), s32[]{:S(2)}) async-start(), calls=%async_computation.6 | async-start | bytes 9437184 | tf_op jit(solution)/shard_map/all_gather | solution.py:88
Sparse Core Ops, SparseCore 0:
  111.8 19.7 reduce-scatter.2
  134.1 80.5 reduce-scatter.4
  220.9 63.8 all-gather.3
  289.4 112.6 all-gather.5
